TPU v7x, 256 devices: a whole 4x4x8 slice. The times are simulated.
256 devices in a mesh: rows: 8 (over y, core), cols: 32 (over x, z).
Axes of the slice: x: 4, y: 4, z: 8, core: 2. Of those that a mesh axis runs over, the one named last changes fastest.
Arguments:
- logged: bfloat16 [32768, 128], P(('rows', 'cols')), may hold values from -5 to 5
- targets: bfloat16 [65536, 128], P('cols'), may hold values from -5 to 5
- log_a: float32 [32768], P('rows'), may hold values from -2 to 2
- log_b: float32 [65536], P('cols'), may hold values from -2 to 2
- start_g: float32 [65536], P('cols'), may hold values from -2 to 142
Outputs:
- pot_f: float32 [32768], P('rows')
- pot_g: float32 [65536], P('cols')
All inputs are finite; a program needn't handle non-finite values.
Results may differ from a plain program's by a relative error of at most 0.0003.
Values may be sent and summed in bfloat16 or wider, within the bound.
A program may use at most 64 MiB of HBM per device.

v0:
```python
import jax
import jax.numpy as jnp
from jax import lax
from jax.sharding import PartitionSpec as P

ITERS = 3
EPS = 0.5
BLOCK = 256


def inner_cost(xb, targets, tnorm):
    xnorm = jnp.sum(jnp.square(xb.astype(jnp.float32)), axis=1)
    inner = lax.dot_general(
        xb, targets, (((1,), (1,)), ((), ())), preferred_element_type=jnp.float32
    )
    return xnorm[:, None] + tnorm[None, :] - 2.0 * inner


def row_partial(x_piece, targets, tnorm, log_b, pot_g):

    def one(xb):
        cost = inner_cost(xb, targets, tnorm)
        s = log_b[None, :] + (pot_g[None, :] - cost) / EPS
        top = jnp.max(s, axis=1)
        total = jnp.sum(jnp.exp(s - top[:, None]), axis=1)
        return jnp.stack([top, total])

    count = x_piece.shape[0]
    parts = lax.map(one, x_piece.reshape(count // BLOCK, BLOCK, x_piece.shape[1]))
    return jnp.transpose(parts, (1, 0, 2)).reshape(2, count)


def col_update(carry, x_piece, f_piece, a_piece, targets, tnorm):

    def step(state, item):
        xb, fb, ab = item
        cost = inner_cost(xb, targets, tnorm)
        s = ab[:, None] + (fb[:, None] - cost) / EPS
        upper = jnp.maximum(state[0], jnp.max(s, axis=0))
        total = state[1] * jnp.exp(state[0] - upper) + jnp.sum(jnp.exp(s - upper[None, :]), axis=0)
        return ((upper, total), None)

    count = x_piece.shape[0]
    blocks = count // BLOCK
    items = (
        x_piece.reshape(blocks, BLOCK, x_piece.shape[1]),
        f_piece.reshape(blocks, BLOCK),
        a_piece.reshape(blocks, BLOCK),
    )
    result, unused = lax.scan(step, carry, items)
    return result


def join_cols(top, total):
    upper = lax.pmax(top, "cols")
    whole = lax.psum(total * jnp.exp(top - upper), "cols")
    return -EPS * (upper + jnp.log(whole))


def join_rows(top, total):
    upper = lax.pmax(top, "rows")
    whole = lax.psum(total * jnp.exp(top - upper), "rows")
    return -EPS * (upper + jnp.log(whole))


def local(logged, targets, log_a, log_b, start_g):
    tnorm = jnp.sum(jnp.square(targets.astype(jnp.float32)), axis=1)
    width = targets.shape[0]
    pot_g = start_g
    pot_f = jnp.zeros(log_a.shape, jnp.float32)
    gathered = lax.all_gather(logged, "cols", axis=0, tiled=True)
    for step in range(ITERS):
        partial_value = row_partial(gathered, targets, tnorm, log_b, pot_g)
        pot_f = join_cols(partial_value[0], partial_value[1])
        init = (jnp.full((width,), -1e30, jnp.float32), jnp.zeros((width,), jnp.float32))
        top, total = col_update(init, gathered, pot_f, log_a, targets, tnorm)
        pot_g = join_rows(top, total)
    return (pot_f, pot_g)


def solution(mesh):
    placed = (P(("rows", "cols"), None), P("cols", None), P("rows"), P("cols"), P("cols"))
    return jax.shard_map(
        local, mesh=mesh, in_specs=placed, out_specs=(P("rows"), P("cols")), check_vma=False
    )
```

profile of v0, /device:TPU:1, one launch (start us, length us, event | category | flops | bytes accessed | tf_op | source)
XLA Modules:
  0.0 1307.4 jit_solution(6303000346675965485)
XLA Ops:
  10.1 76.1 %all-gather.2.cloned.1.call-done = bf16[4096,128]{1,0:T(8,128)(2,1)} async-done(((bf16[128,128]{1,0:T(8,128)(2,1)}), bf16[4096,128]{1,0:T(8,128)(2,1)}) %all-gather.2.cloned.1.call-update) | async-done | bytes 1048592 | tf_op jit(solution)/shard_map/all_gather | solution.py:71
  86.2 51.2 %while.69 = (s32[]{:T(128)}, f32[16,2,256]{2,1,0:T(2,128)S(1)}, f32[2048]{0:T(1024)}, f32[2048]{0:T(1024)}, bf16[16,256,128]{2,1,0:T(8,128)(2,1)}, /*index=5*/f3...) while((s32[]{:T(128)}, f32[16,2,256]{2,1,0:T(2,128)S(1)}, f32[2048]{0:T(1024)}, f32[2048]{0:T(1024)}, ...), condition=%wide.region_5.6_spmd, body=%wide.region_1.5_spmd.sunk | while | flops 139034368 | bytes 4884061 | solution.py:29
  90.3 1.8 fusion.82
  93.5 1.8 fusion.82
  96.7 1.8 fusion.82
  99.9 1.8 fusion.82
  103.1 1.8 fusion.82
  106.3 1.8 fusion.82
  109.5 1.8 fusion.82
  112.7 1.8 fusion.82
  115.9 1.8 fusion.82
  119.1 1.8 fusion.82
  122.3 1.8 fusion.82
  125.5 1.8 fusion.82
  128.7 1.8 fusion.82
  137.4 112.5 %pmax.42 = f32[4096]{0:T(1024)S(1)} all-reduce(f32[4096]{0:T(1024)S(1)} %bitcast.143), channel_id=1, replica_groups=mesh['rows'=8,'cols'=32] {'cols'}, use_global_device_ids=true, to_apply=%region_6.7 | all-reduce | flops 4096 | bytes 32768 | tf_op jit(solution)/shard_map/pmax | solution.py:55
  249.9 110.6 %psum.42 = f32[4096]{0:T(1024)S(1)} all-reduce(f32[4096]{0:T(1024)S(1)} %exponential_multiply_fusion.2), channel_id=1, replica_groups=mesh['rows'=8,'cols'=32] {'cols'}, use_global_device_ids=true, to_apply=%region_7.8 | all-reduce | flops 4096 | bytes 32768 | tf_op jit(solution)/shard_map/psum | solution.py:56
  360.5 49.6 %while.72 = (s32[]{:T(128)}, f32[2048]{0:T(1024)S(1)}, f32[2048]{0:T(1024)S(1)}, f32[16,256]{1,0:T(8,128)S(1)}, f32[16,256]{1,0:T(8,128)S(1)}, /*index=5*/bf16[1...) while((s32[]{:T(128)}, f32[2048]{0:T(1024)S(1)}, ...), condition=%wide.region_12.13_spmd.clone, body=%wide.region_8.12_spmd.clone.sunk | while | flops 139044608 | bytes 4973176 | solution.py:50
  410.1 72.0 %pmax.43 = f32[2048]{0:T(1024)S(1)} all-reduce(f32[2048]{0:T(1024)S(1)} %get-tuple-element.243), channel_id=1, replica_groups=mesh['rows'=8,'cols'=32] {'rows'}, use_global_device_ids=true, to_apply=%region_13.14 | all-reduce | flops 2048 | bytes 16384 | tf_op jit(solution)/shard_map/pmax | solution.py:61
  482.1 12.7 psum.43
  494.8 51.9 %while.70 = (s32[]{:T(128)}, f32[16,2,256]{2,1,0:T(2,128)S(1)}, f32[2048]{0:T(1024)S(1)}, f32[2048]{0:T(1024)S(1)}, bf16[16,256,128]{2,1,0:T(8,128)(2,1)}, /*ind...) while((s32[]{:T(128)}, f32[16,2,256]{2,1,0:T(2,128)S(1)}, f32[2048]{0:T(1024)S(1)}, ...), condition=%wide.region_19.20_spmd, body=%wide.region_15.19_spmd.sunk | while | flops 139034368 | bytes 4884061 | solution.py:29
  495.8 1.8 fusion.85
  499.0 1.8 fusion.85
  502.3 1.8 fusion.85
  505.5 1.8 fusion.85
  508.8 1.8 fusion.85
  512.0 1.8 fusion.85
  515.3 1.8 fusion.85
  518.5 1.8 fusion.85
  521.8 1.8 fusion.85
  525.0 1.8 fusion.85
  528.3 1.8 fusion.85
  531.5 1.8 fusion.85
  534.7 1.8 fusion.85
  538.0 1.8 fusion.85
  541.2 1.8 fusion.85
  544.5 1.8 fusion.85
  546.8 109.9 %pmax.44 = f32[4096]{0:T(1024)S(1)} all-reduce(f32[4096]{0:T(1024)S(1)} %bitcast.145), channel_id=1, replica_groups=mesh['rows'=8,'cols'=32] {'cols'}, use_global_device_ids=true, to_apply=%region_20.21 | all-reduce | flops 4096 | bytes 32768 | tf_op jit(solution)/shard_map/pmax | solution.py:55
  656.7 110.3 %psum.44 = f32[4096]{0:T(1024)S(1)} all-reduce(f32[4096]{0:T(1024)S(1)} %exponential_multiply_fusion.1), channel_id=1, replica_groups=mesh['rows'=8,'cols'=32] {'cols'}, use_global_device_ids=true, to_apply=%region_21.22 | all-reduce | flops 4096 | bytes 32768 | tf_op jit(solution)/shard_map/psum | solution.py:56
  767.0 49.6 %while.73 = (s32[]{:T(128)}, f32[2048]{0:T(1024)S(1)}, f32[2048]{0:T(1024)S(1)}, f32[16,256]{1,0:T(8,128)S(1)}, f32[16,256]{1,0:T(8,128)S(1)}, /*index=5*/bf16[1...) while((s32[]{:T(128)}, f32[2048]{0:T(1024)S(1)}, ...), condition=%wide.region_26.27_spmd.clone, body=%wide.region_22.26_spmd.clone.sunk | while | flops 139044608 | bytes 4973176 | solution.py:50
  816.6 67.8 %pmax.45 = f32[2048]{0:T(1024)S(1)} all-reduce(f32[2048]{0:T(1024)S(1)} %get-tuple-element.246), channel_id=1, replica_groups=mesh['rows'=8,'cols'=32] {'rows'}, use_global_device_ids=true, to_apply=%region_27.28 | all-reduce | flops 2048 | bytes 16384 | tf_op jit(solution)/shard_map/pmax | solution.py:61
  884.4 12.7 psum.45
  897.2 51.8 %while.71 = (s32[]{:T(128)}, f32[16,2,256]{2,1,0:T(2,128)S(1)}, f32[2048]{0:T(1024)S(1)}, f32[2048]{0:T(1024)S(1)}, bf16[16,256,128]{2,1,0:T(8,128)(2,1)}, /*ind...) while((s32[]{:T(128)}, f32[16,2,256]{2,1,0:T(2,128)S(1)}, f32[2048]{0:T(1024)S(1)}, ...), condition=%wide.region_33.34_spmd, body=%wide.region_29.33_spmd.sunk | while | flops 139034368 | bytes 4884061 | solution.py:29
  898.1 1.8 fusion.88
  901.4 1.8 fusion.88
  904.6 1.8 fusion.88
  907.8 1.8 fusion.88
  911.1 1.8 fusion.88
  914.3 1.8 fusion.88
  917.6 1.8 fusion.88
  920.8 1.8 fusion.88
  924.0 1.8 fusion.88
  927.3 1.8 fusion.88
  930.5 1.8 fusion.88
  933.8 1.8 fusion.88
  937.0 1.8 fusion.88
  940.2 1.8 fusion.88
  943.5 1.8 fusion.88
  946.7 1.8 fusion.88
  949.0 109.9 %pmax.46 = f32[4096]{0:T(1024)S(1)} all-reduce(f32[4096]{0:T(1024)S(1)} %bitcast.147), channel_id=1, replica_groups=mesh['rows'=8,'cols'=32] {'cols'}, use_global_device_ids=true, to_apply=%region_34.35 | all-reduce | flops 4096 | bytes 32768 | tf_op jit(solution)/shard_map/pmax | solution.py:55
  1059.0 110.3 %psum.46 = f32[4096]{0:T(1024)S(1)} all-reduce(f32[4096]{0:T(1024)S(1)} %exponential_multiply_fusion), channel_id=1, replica_groups=mesh['rows'=8,'cols'=32] {'cols'}, use_global_device_ids=true, to_apply=%region_35.36 | all-reduce | flops 4096 | bytes 32768 | tf_op jit(solution)/shard_map/psum | solution.py:56
  1169.9 49.6 %while.74 = (s32[]{:T(128)}, f32[2048]{0:T(1024)S(1)}, f32[2048]{0:T(1024)S(1)}, f32[16,256]{1,0:T(8,128)S(1)}, f32[16,256]{1,0:T(8,128)S(1)}, /*index=5*/bf16[1...) while((s32[]{:T(128)}, f32[2048]{0:T(1024)S(1)}, ...), condition=%wide.region_40.41_spmd.clone, body=%wide.region_36.40_spmd.clone.sunk | while | flops 139044608 | bytes 4973176 | solution.py:50
  1219.5 67.8 %pmax.47 = f32[2048]{0:T(1024)S(1)} all-reduce(f32[2048]{0:T(1024)S(1)} %get-tuple-element.249), channel_id=1, replica_groups=mesh['rows'=8,'cols'=32] {'rows'}, use_global_device_ids=true, to_apply=%region_41.42 | all-reduce | flops 2048 | bytes 16384 | tf_op jit(solution)/shard_map/pmax | solution.py:61
  1287.3 12.7 psum.47
  (518 shorter events, 223.5 us)
Async XLA Ops:
  7.2 79.0 %all-gather.2.cloned.1.call-start = ((), (), s32[]{:S(2)}) async-start(), calls=%async_computation | async-start | bytes 1081344 | tf_op jit(solution)/shard_map/all_gather | solution.py:71
  360.5 134.3 %copy-start.1 = (f32[2048]{0:T(1024)S(1)}, f32[2048]{0:T(1024)}, u32[]{:S(2)}) copy-start(f32[2048]{0:T(1024)} %get-tuple-element.941) | copy-start | bytes 24580
  1169.3 0.6 copy-start
Sparse Core Ops, SparseCore 0:
  10.6 75.5 all-gather.1
where the time goes:
time: 1310 us
  blocking collectives  909 us (69%)
  matrix products  170 us (13%)
  other arithmetic  131 us (10%)
  waiting for transfers between devices  76.8 us (6%)
  between operations  14.3 us (1%)
    pmax x3, blocking collectives, join_cols(): upper = lax.pmax(top, 'cols')  332 us
    psum x3, blocking collectives, join_cols(): whole = lax.psum(total * jnp.exp(top - upper), 'cols')  331 us
    pmax x3, blocking collectives, join_rows(): upper = lax.pmax(top, 'rows')  208 us
    dot_general x96, matrix products, inner_cost(): lax.dot_general(xb, targets, (((1,), (1,)), ((), ())), preferred_element_...  170 us
    reduce_sum x96, other arithmetic, inner_cost(): xnorm = jnp.sum(jnp.square(xb.astype(jnp.float32)), axis=1)  91.7 us
    all_gather x1, waiting for transfers between devices, local(): gathered = lax.all_gather(logged, 'cols', axis=0, tiled=True)  76.1 us
    psum x3, blocking collectives, join_rows(): whole = lax.psum(total * jnp.exp(top - upper), 'rows')  38 us
  transfers between devices with their start and end apart: 1, of which 1 were waited for; matrix products, arithmetic and copies ran while one was open for 0% of the time, Pallas kernels for 0%

commit v1 on v0

--- a/solution.py
+++ b/solution.py
@@ -68,7 +68,10 @@
     width = targets.shape[0]
     pot_g = start_g
     pot_f = jnp.zeros(log_a.shape, jnp.float32)
-    gathered = lax.all_gather(logged, "cols", axis=0, tiled=True)
+    size = lax.axis_size("cols")
+    shards = jnp.stack([logged for _ in range(size)])
+    shards = lax.all_to_all(shards, "cols", split_axis=0, concat_axis=0)
+    gathered = jnp.concatenate(shards, axis=0)
     for step in range(ITERS):
         partial_value = row_partial(gathered, targets, tnorm, log_b, pot_g)
         pot_f = join_cols(partial_value[0], partial_value[1])

time: 1310 us -> 1170 us (0.89)
  other arithmetic: 131 us -> 51.2 us
  waiting for transfers between devices: 76.8 us -> 23.2 us
  between operations: 14.3 us -> 0.98 us
    reduce_sum x96, other arithmetic: 91.7 us -> 11.4 us  [inner_cost(): xnorm = jnp.sum(jnp.square(xb.astype(jnp.float32)), axis=1)]
    all_gather x1 -> x0, waiting for transfers between devices: 76.1 us -> none  [local(): gathered = lax.all_gather(logged, 'cols', axis=0, tiled=True)]
    all_to_all x0 -> x1, waiting for transfers between devices: none -> 23.2 us  [local(): shards = lax.all_to_all(shards, 'cols', split_axis=0, concat_axis=0)]
where the time goes in v1:
time: 1170 us
  blocking collectives  909 us (78%)
  matrix products  167 us (14%)
  other arithmetic  51.2 us (4%)
  waiting for transfers between devices  23.2 us (2%)
  starting transfers between devices  11.9 us (1%)
    pmax x3, blocking collectives, join_cols(): upper = lax.pmax(top, 'cols')  335 us
    psum x3, blocking collectives, join_cols(): whole = lax.psum(total * jnp.exp(top - upper), 'cols')  331 us
    pmax x3, blocking collectives, join_rows(): upper = lax.pmax(top, 'rows')  205 us
    dot_general x96, matrix products, inner_cost(): lax.dot_general(xb, targets, (((1,), (1,)), ((), ())), preferred_element_...  167 us
    psum x3, blocking collectives, join_rows(): whole = lax.psum(total * jnp.exp(top - upper), 'rows')  37.8 us
  transfers between devices with their start and end apart: 1, of which 1 were waited for; matrix products, arithmetic and copies ran while one was open for 0% of the time, Pallas kernels for 0%

profile of v1, /device:TPU:1, one launch (start us, length us, event | category | flops | bytes accessed | tf_op | source)
XLA Modules:
  0.0 1169.8 jit_solution(619571775580261562)
XLA Ops:
  0.7 2.0 stack.20
  2.7 11.9 %all-to-all-start = ((bf16[32,128,128]{2,1,0:T(8,128)(2,1)}), bf16[32,128,128]{2,1,0:T(8,128)(2,1)S(1)}, u32[]{:S(2)}, u32[]{:S(2)}) async-start(bf16[32,128,128]{2,1,0:T(8,128)(2,1)} %stack.20), calls=%async_computation | async-start | bytes 2097152 | tf_op jit(solution)/shard_map/all_to_all | solution.py:73
  16.0 23.2 %all-to-all-done = bf16[32,128,128]{2,1,0:T(8,128)(2,1)S(1)} async-done(((bf16[32,128,128]{2,1,0:T(8,128)(2,1)}), bf16[32,128,128]{2,1,0:T(8,128)(2,1)S(1)}, u32[]{:S(2)}, u32[]{:S(2)}) %all-to-all-start) | async-done | bytes 1048608 | tf_op jit(solution)/shard_map/all_to_all | solution.py:73
  39.2 37.9 %while.69 = (s32[]{:T(128)}, f32[16,2,256]{2,1,0:T(2,128)S(1)}, f32[2048]{0:T(1024)S(1)}, f32[2048]{0:T(1024)S(1)}, bf16[16,256,128]{2,1,0:T(8,128)(2,1)S(1)}, /...) while((s32[]{:T(128)}, f32[16,2,256]{2,1,0:T(2,128)S(1)}, f32[2048]{0:T(1024)S(1)}, ...), condition=%wide.region_5.6_spmd, body=%wide.region_1.5_spmd.sunk | while | flops 139034368 | bytes 4883553 | solution.py:29
  44.1 1.8 fusion.82
  48.8 1.8 fusion.82
  51.2 1.8 fusion.82
  53.5 1.8 fusion.82
  55.9 1.8 fusion.82
  58.2 1.8 fusion.82
  60.6 1.8 fusion.82
  63.0 1.8 fusion.82
  65.3 1.8 fusion.82
  70.1 1.8 fusion.82
  72.4 1.8 fusion.82
  77.1 114.7 %pmax.42 = f32[4096]{0:T(1024)S(1)} all-reduce(f32[4096]{0:T(1024)S(1)} %bitcast.143), channel_id=1, replica_groups=mesh['rows'=8,'cols'=32] {'cols'}, use_global_device_ids=true, to_apply=%region_6.7 | all-reduce | flops 4096 | bytes 32768 | tf_op jit(solution)/shard_map/pmax | solution.py:55
  191.8 110.6 %psum.42 = f32[4096]{0:T(1024)S(1)} all-reduce(f32[4096]{0:T(1024)S(1)} %exponential_multiply_fusion.2), channel_id=1, replica_groups=mesh['rows'=8,'cols'=32] {'cols'}, use_global_device_ids=true, to_apply=%region_7.8 | all-reduce | flops 4096 | bytes 32768 | tf_op jit(solution)/shard_map/psum | solution.py:56
  302.4 35.6 %while.72 = (s32[]{:T(128)}, f32[2048]{0:T(1024)S(1)}, f32[2048]{0:T(1024)S(1)}, f32[16,256]{1,0:T(8,128)S(1)}, f32[16,256]{1,0:T(8,128)S(1)}, /*index=5*/bf16[1...) while((s32[]{:T(128)}, f32[2048]{0:T(1024)S(1)}, ...), condition=%wide.region_12.13_spmd.clone, body=%wide.region_8.12_spmd.clone.sunk | while | flops 139044608 | bytes 4972668 | solution.py:50
  338.0 69.4 %pmax.43 = f32[2048]{0:T(1024)S(1)} all-reduce(f32[2048]{0:T(1024)S(1)} %get-tuple-element.243), channel_id=1, replica_groups=mesh['rows'=8,'cols'=32] {'rows'}, use_global_device_ids=true, to_apply=%region_13.14 | all-reduce | flops 2048 | bytes 16384 | tf_op jit(solution)/shard_map/pmax | solution.py:61
  407.5 12.5 %psum.43 = f32[2048]{0:T(1024)S(1)} all-reduce(f32[2048]{0:T(1024)S(1)} %exponential_multiply_fusion.5), channel_id=1, replica_groups=mesh['rows'=8,'cols'=32] {'rows'}, use_global_device_ids=true, to_apply=%region_14.15 | all-reduce | flops 2048 | bytes 16384 | tf_op jit(solution)/shard_map/psum | solution.py:62
  420.0 37.9 %while.70 = (s32[]{:T(128)}, f32[16,2,256]{2,1,0:T(2,128)S(1)}, f32[2048]{0:T(1024)S(1)}, f32[2048]{0:T(1024)S(1)}, bf16[16,256,128]{2,1,0:T(8,128)(2,1)S(1)}, /...) while((s32[]{:T(128)}, f32[16,2,256]{2,1,0:T(2,128)S(1)}, f32[2048]{0:T(1024)S(1)}, ...), condition=%wide.region_19.20_spmd, body=%wide.region_15.19_spmd.sunk | while | flops 139034368 | bytes 4883553 | solution.py:29
  420.2 1.8 fusion.85
  422.5 1.8 fusion.85
  424.9 1.8 fusion.85
  427.3 1.8 fusion.85
  429.6 1.8 fusion.85
  432.0 1.8 fusion.85
  434.4 1.8 fusion.85
  436.7 1.8 fusion.85
  439.1 1.8 fusion.85
  441.5 1.8 fusion.85
  443.8 1.8 fusion.85
  446.2 1.8 fusion.85
  448.6 1.8 fusion.85
  450.9 1.8 fusion.85
  453.3 1.8 fusion.85
  455.6 1.8 fusion.85
  457.9 110.0 %pmax.44 = f32[4096]{0:T(1024)S(1)} all-reduce(f32[4096]{0:T(1024)S(1)} %bitcast.145), channel_id=1, replica_groups=mesh['rows'=8,'cols'=32] {'cols'}, use_global_device_ids=true, to_apply=%region_20.21 | all-reduce | flops 4096 | bytes 32768 | tf_op jit(solution)/shard_map/pmax | solution.py:55
  567.9 110.3 %psum.44 = f32[4096]{0:T(1024)S(1)} all-reduce(f32[4096]{0:T(1024)S(1)} %exponential_multiply_fusion.1), channel_id=1, replica_groups=mesh['rows'=8,'cols'=32] {'cols'}, use_global_device_ids=true, to_apply=%region_21.22 | all-reduce | flops 4096 | bytes 32768 | tf_op jit(solution)/shard_map/psum | solution.py:56
  678.2 35.6 %while.73 = (s32[]{:T(128)}, f32[2048]{0:T(1024)S(1)}, f32[2048]{0:T(1024)S(1)}, f32[16,256]{1,0:T(8,128)S(1)}, f32[16,256]{1,0:T(8,128)S(1)}, /*index=5*/bf16[1...) while((s32[]{:T(128)}, f32[2048]{0:T(1024)S(1)}, ...), condition=%wide.region_26.27_spmd.clone, body=%wide.region_22.26_spmd.clone.sunk | while | flops 139044608 | bytes 4972668 | solution.py:50
  713.8 67.8 %pmax.45 = f32[2048]{0:T(1024)S(1)} all-reduce(f32[2048]{0:T(1024)S(1)} %get-tuple-element.246), channel_id=1, replica_groups=mesh['rows'=8,'cols'=32] {'rows'}, use_global_device_ids=true, to_apply=%region_27.28 | all-reduce | flops 2048 | bytes 16384 | tf_op jit(solution)/shard_map/pmax | solution.py:61
  781.7 12.7 %psum.45 = f32[2048]{0:T(1024)S(1)} all-reduce(f32[2048]{0:T(1024)S(1)} %exponential_multiply_fusion.4), channel_id=1, replica_groups=mesh['rows'=8,'cols'=32] {'rows'}, use_global_device_ids=true, to_apply=%region_28.29 | all-reduce | flops 2048 | bytes 16384 | tf_op jit(solution)/shard_map/psum | solution.py:62
  794.4 37.9 %while.71 = (s32[]{:T(128)}, f32[16,2,256]{2,1,0:T(2,128)S(1)}, f32[2048]{0:T(1024)S(1)}, f32[2048]{0:T(1024)S(1)}, bf16[16,256,128]{2,1,0:T(8,128)(2,1)S(1)}, /...) while((s32[]{:T(128)}, f32[16,2,256]{2,1,0:T(2,128)S(1)}, f32[2048]{0:T(1024)S(1)}, ...), condition=%wide.region_33.34_spmd, body=%wide.region_29.33_spmd.sunk | while | flops 139034368 | bytes 4883553 | solution.py:29
  794.5 1.8 fusion.88
  796.9 1.8 fusion.88
  799.2 1.8 fusion.88
  801.6 1.8 fusion.88
  804.0 1.8 fusion.88
  806.3 1.8 fusion.88
  808.7 1.8 fusion.88
  811.1 1.8 fusion.88
  813.4 1.8 fusion.88
  815.8 1.8 fusion.88
  818.2 1.8 fusion.88
  820.5 1.8 fusion.88
  822.9 1.8 fusion.88
  825.3 1.8 fusion.88
  827.6 1.8 fusion.88
  830.0 1.8 fusion.88
  832.3 109.9 %pmax.46 = f32[4096]{0:T(1024)S(1)} all-reduce(f32[4096]{0:T(1024)S(1)} %bitcast.147), channel_id=1, replica_groups=mesh['rows'=8,'cols'=32] {'cols'}, use_global_device_ids=true, to_apply=%region_34.35 | all-reduce | flops 4096 | bytes 32768 | tf_op jit(solution)/shard_map/pmax | solution.py:55
  942.2 110.3 %psum.46 = f32[4096]{0:T(1024)S(1)} all-reduce(f32[4096]{0:T(1024)S(1)} %exponential_multiply_fusion), channel_id=1, replica_groups=mesh['rows'=8,'cols'=32] {'cols'}, use_global_device_ids=true, to_apply=%region_35.36 | all-reduce | flops 4096 | bytes 32768 | tf_op jit(solution)/shard_map/psum | solution.py:56
  1053.1 35.6 %while.74 = (s32[]{:T(128)}, f32[2048]{0:T(1024)S(1)}, f32[2048]{0:T(1024)S(1)}, f32[16,256]{1,0:T(8,128)S(1)}, f32[16,256]{1,0:T(8,128)S(1)}, /*index=5*/bf16[1...) while((s32[]{:T(128)}, f32[2048]{0:T(1024)S(1)}, ...), condition=%wide.region_40.41_spmd.clone, body=%wide.region_36.40_spmd.clone.sunk | while | flops 139044608 | bytes 4972668 | solution.py:50
  1088.7 67.8 %pmax.47 = f32[2048]{0:T(1024)S(1)} all-reduce(f32[2048]{0:T(1024)S(1)} %get-tuple-element.249), channel_id=1, replica_groups=mesh['rows'=8,'cols'=32] {'rows'}, use_global_device_ids=true, to_apply=%region_41.42 | all-reduce | flops 2048 | bytes 16384 | tf_op jit(solution)/shard_map/pmax | solution.py:61
  1156.5 12.7 %psum.47 = f32[2048]{0:T(1024)S(1)} all-reduce(f32[2048]{0:T(1024)S(1)} %exponential_multiply_fusion.3), channel_id=1, replica_groups=mesh['rows'=8,'cols'=32] {'rows'}, use_global_device_ids=true, to_apply=%region_42.43 | all-reduce | flops 2048 | bytes 16384 | tf_op jit(solution)/shard_map/psum | solution.py:62
  (522 shorter events, 143.5 us)
Async XLA Ops:
  0.6 14.0 %copy-start.1 = (f32[4096]{0:T(1024)S(1)}, f32[4096]{0:T(1024)}, u32[]{:S(2)}) copy-start(f32[4096]{0:T(1024)} %param.19) | copy-start | bytes 49156
  0.6 38.5 %copy-start.3 = (f32[2048]{0:T(1024)S(1)}, f32[2048]{0:T(1024)}, u32[]{:S(2)}) copy-start(f32[2048]{0:T(1024)} %param.20) | copy-start | bytes 24580
  0.7 38.5 %copy-start.2 = (f32[2048]{0:T(1024)S(1)}, f32[2048]{0:T(1024)}, u32[]{:S(2)}) copy-start(f32[2048]{0:T(1024)} %param.21) | copy-start | bytes 24580
  2.7 36.5 %all-to-all-start = ((bf16[32,128,128]{2,1,0:T(8,128)(2,1)}), bf16[32,128,128]{2,1,0:T(8,128)(2,1)S(1)}, u32[]{:S(2)}, u32[]{:S(2)}) async-start(bf16[32,128,128]{2,1,0:T(8,128)(2,1)} %stack.20), calls=%async_computation | async-start | bytes 2097152 | tf_op jit(solution)/shard_map/all_to_all | solution.py:73
  1052.5 0.6 copy-start
